TPU v7x, 512 devices: a whole 4x4x16 slice. The times are simulated.
512 devices in a mesh: line: 32 (over x, y, core), seg: 16 (over z).
Axes of the slice: x: 4, y: 4, z: 16, core: 2. Of those that a mesh axis runs over, the one named last changes fastest.
Arguments:
- points: float32 [32, 16, 3, 32768], P('line', 'seg'), may hold values from -1 to 1
- rows: int32 [32, 16, 2, 3072], P('line', 'seg'), may hold values from -1 to 32767, as said below
- cells: int32 [32, 16, 2, 24], P('line', 'seg'), may hold values from -1 to 15, as said below
- pose: float32 [12, 32], P(None, 'line'), as said below
Outputs:
- matched: float32 [32, 16, 2, 5, 3072], P('line', 'seg')
- fitted_pose: float32 [12, 32], P(None, 'line')
- final_spread: float32 [1], replicated
Inputs may be any that keep to these rules, and one draw needn't show every extreme that they name: In each block of 128 slots the filled slots come first; every slot of an empty block is empty; rows toward the lower line lie in the lower margin (below 8192), rows toward the upper line in the upper margin (24576 or more); the lists of line 0 toward the lower side and of line 32 - 1 toward the upper side are empty. `cells`: empty blocks come after the others; in segment 0 of every line all blocks toward an existing adjacent line are filled. `pose`: every 3x3 part is within about 0.5 of the identity.
All inputs are finite; a program needn't handle non-finite values.
Results may differ from a plain program's by a relative error of at most 0.0003.
Values sent between devices are 32-bit elements; how exact they have to be, the bound alone decides.
A program may use at most 64 MiB of HBM per device.

v0:
```python
import jax
import jax.numpy as jnp
from jax import lax
from jax.sharding import PartitionSpec as P

NCELL = 16
CT = 512
BLOCK = 128
ITERS = 2
OUTLIER_MASS = 1.0
SPREAD_START = 0.05
PRIOR_TOP = 0.05
PRIOR_BOTTOM = 1.0
REGULARIZE = 1.0
blocks_per_turn = 4


def from_behind(value, axis, steps):
    count = lax.axis_size(axis)
    initial, last = (max(0, -steps), min(count, count - steps))
    return lax.ppermute(value, axis, [(source, source + steps) for source in range(initial, last)])


def match_block(source_block, cell_id, world_points, spread):
    first_column = jnp.maximum(cell_id, 0) * CT
    target = lax.dynamic_slice_in_dim(world_points, first_column, CT, 1)
    distance = (source_block[0][:, None] - target[0][None, :]) ** 2
    distance = distance + (source_block[1][:, None] - target[1][None, :]) ** 2
    distance = distance + (source_block[2][:, None] - target[2][None, :]) ** 2
    weight = jnp.exp(-distance / (2.0 * spread))
    total_weight = jnp.sum(weight, axis=1)
    posterior = weight / (total_weight + OUTLIER_MASS)[:, None]
    pulled = lax.dot_general(
        target,
        posterior,
        (((1,), (1,)), ((), ())),
        precision=lax.Precision.HIGHEST,
        preferred_element_type=jnp.float32,
    )
    share_row = total_weight / (total_weight + OUTLIER_MASS)
    energy_row = jnp.sum(posterior * distance, axis=1)
    merged_rows = jnp.concatenate([pulled, share_row[None, :], energy_row[None, :]], axis=0)
    return jnp.where(cell_id >= 0, merged_rows, jnp.zeros_like(merged_rows))


def match_all(sources, block_cells, worlds, spread):
    block_total = block_cells.shape[1]
    turns = 2 * block_total // blocks_per_turn
    grouped = (
        sources.reshape(2, 3, block_total, BLOCK)
        .transpose(0, 2, 1, 3)
        .reshape(turns, blocks_per_turn, 3, BLOCK)
    )
    grouped_cells = block_cells.reshape(turns, blocks_per_turn)
    sides = jnp.arange(turns) // (turns // 2)

    def one_turn(packed):
        turn_blocks, turn_cells, side = packed
        target_world = lax.dynamic_index_in_dim(worlds, side, 0, keepdims=False)

        def compute(unused):
            return jax.vmap(
                lambda block_points, block_cell: match_block(
                    block_points, block_cell, target_world, spread
                )
            )(turn_blocks, turn_cells)

        def skipped(unused):
            return jnp.zeros((blocks_per_turn, 5, BLOCK), jnp.float32)

        return lax.cond(jnp.any(turn_cells >= 0), compute, skipped, 0)

    output = lax.map(one_turn, (grouped, grouped_cells, sides))
    return (
        output.reshape(2, block_total, 5, BLOCK)
        .transpose(0, 2, 1, 3)
        .reshape(2, 5, block_total * BLOCK)
    )


def solve_pose(gram_matrix, cross_matrix, pose_column):
    old_pose = jnp.concatenate(
        [pose_column[:9].reshape(3, 3), pose_column[9:].reshape(3, 1)], axis=1
    )
    left_side = gram_matrix + REGULARIZE * jnp.eye(4, dtype=gram_matrix.dtype)
    right_side = cross_matrix + REGULARIZE * old_pose
    factor = jnp.linalg.cholesky(left_side)
    solved = jax.scipy.linalg.cho_solve((factor, True), right_side.T)
    new_pose = solved.T
    return jnp.concatenate([new_pose[:, :3].reshape(9), new_pose[:, 3]])


def send_lists(lists, marks, step):
    return from_behind((lists, marks), "line", step)


def send_back(piece, step):
    return from_behind(piece, "line", step)


def on_device(points, rows, cells, pose):
    own_points = points[0, 0]
    row_list = rows[0, 0]
    cell_ids = cells[0, 0]
    pose_column = pose[:, 0]
    margin = NCELL * CT
    point_total = own_points.shape[1]
    slot_total = row_list.shape[1]
    live_slots = (row_list >= 0).astype(jnp.float32)
    safe_rows = jnp.where(row_list >= 0, row_list, 0)
    raw_source = (
        jnp.take(own_points, safe_rows.reshape(-1), axis=1)
        .reshape(3, 2, slot_total)
        .transpose(1, 0, 2)
    )
    extended = jnp.concatenate([raw_source, jnp.ones((2, 1, slot_total), jnp.float32)], axis=1)
    spread = jnp.float32(SPREAD_START)
    result = None
    for iteration in range(ITERS):
        linear_part = pose_column[:9].reshape(3, 3)
        offset_part = pose_column[9:]
        world_points = (
            jnp.dot(
                linear_part,
                own_points,
                precision=lax.Precision.HIGHEST,
                preferred_element_type=jnp.float32,
            )
            + offset_part[:, None]
        )
        moved_source = (
            jnp.einsum("km,dms->dks", linear_part, raw_source, precision=lax.Precision.HIGHEST)
            + offset_part[None, :, None]
        )
        lower_margin = world_points[:, :margin]
        upper_margin = world_points[:, point_total - margin :]
        cell_marks = (cell_ids + 1).astype(jnp.float32)
        lists_down, marks_down = send_lists(moved_source[0], cell_marks[0], -1)
        lists_up, marks_up = send_lists(moved_source[1], cell_marks[1], 1)
        incoming = jnp.stack([lists_down, lists_up])
        got_cells = jnp.stack([marks_down, marks_up]).astype(jnp.int32) - 1
        own_worlds = jnp.stack([upper_margin, lower_margin])
        answers = match_all(incoming, got_cells, own_worlds, spread)
        result = jnp.stack([send_back(answers[0], 1), send_back(answers[1], -1)])
        result = result * live_slots[:, None, :]
        pulled = result[:, :3]
        share_all = result[:, 3]
        energy_all = result[:, 4]
        gram_matrix = jnp.einsum(
            "dks,dms->km",
            extended * share_all[:, None, :],
            extended,
            precision=lax.Precision.HIGHEST,
        )
        cross_matrix = jnp.einsum("dks,dms->km", pulled, extended, precision=lax.Precision.HIGHEST)
        energy_part = jnp.sum(energy_all)
        share_part = jnp.sum(share_all)
        gram_sum, cross_sum = lax.psum((gram_matrix, cross_matrix), "seg")
        energy_sum, share_sum = lax.psum((energy_part, share_part), ("line", "seg"))
        pose_column = solve_pose(gram_sum, cross_sum, pose_column)
        spread = (energy_sum + PRIOR_TOP) / (3.0 * share_sum + PRIOR_BOTTOM)
    return (result[None, None], pose_column[:, None], spread.reshape(1))


def solution(mesh):
    return jax.shard_map(
        on_device,
        mesh=mesh,
        in_specs=(
            P("line", "seg", None, None),
            P("line", "seg", None, None),
            P("line", "seg", None, None),
            P(None, "line"),
        ),
        out_specs=(P("line", "seg", None, None, None), P(None, "line"), P()),
        check_vma=False,
    )
```

profile of v0, /device:TPU:2, one launch (start us, length us, event | category | flops | bytes accessed | tf_op | source)
XLA Modules:
  0.0 667.9 jit_solution(6395573650611481252)
XLA Ops:
  13.1 21.8 %gather_fusion = f32[6144,3]{1,0:T(8,128)S(1)} fusion(f32[3,32768]{0,1:T(8,128)} %bitcast.285, s32[6144]{0:T(1024)S(1)} %broadcast_clamp_fusion), kind=kCustom, calls=%fused_computation | custom fusion | bytes 172032 | tf_op jit(solution)/shard_map/jit(_take)/gather | solution.py:112
  48.7 16.7 %convolution_add_fusion.1 = f32[3,32768]{1,0:T(4,128)S(1)} fusion(f32[3,3]{1,0:T(4,128)S(1)} %reshape.263, f32[3]{0:T(128)S(1)} %get-tuple-element.442, f32[1,1,3,32768]{2,3,1,0:T(8,128)} %copy.18), kind=kOutput, calls=%fused_computation.61 | convolution fusion | flops 3637248 | bytes 786480 | tf_op jit(solution)/shard_map/dot_general | solution.py:123
  65.8 139.7 %while.28 = (s32[]{:T(128)}, f32[12,4,5,128]{3,2,1,0:T(8,128)S(1)}, s32[12,4]{1,0:T(8,128)S(1)}, f32[2,3,8192]{2,1,0:T(4,128)S(1)}, f32[12,4,3,128]{3,1,2,0:T(4,128)S(1)}, /*index=5*/s32[]{:T(128)}, s32[]{:T(128)}, s32[]{:T(128)}) while((s32[]{:T(128)}, f32[12,4,5,128]{3,2,1,0:T(8,128)S(1)}, s32[12,4]{1,0:T(8,128)S(1)}, ...), condition=%wide.region_6.7_spmd.clone, body=%wide.region_0.6_spmd.clone.sunk | while | flops 18620548 | bytes 529362 | solution.py:73
  67.1 10.3 %conditional.6 = (f32[1,4,5,128]{3,2,1,0:T(8,128)S(1)}) conditional(s32[]{:T(128)} %convert_element_type.49, () %tuple.138, (s32[4]{0:T(128)S(1)}, s32[12]{0:T(128)S(1)}, s32[]{:T(128)}, f32[2,3,8192]{2,1,0:T(4,128)S(1)}, f32[12,4,3,128]{3,1,2,0:T(4,128)S(1)}, /*index=5*/s32[12]{0:T(128)S(1)}, s32[12]{0:T(128)S(1)}, s32[12]{0:T(128)S(1)}, ...), branch_computations={%region_2.2_spmd, %region_3.5_spmd.clone} | conditional | flops 18620528 | bytes 496227 | solution.py:71
  78.7 10.3 %conditional.6 = (f32[1,4,5,128]{3,2,1,0:T(8,128)S(1)}) conditional(s32[]{:T(128)} %convert_element_type.49, () %tuple.138, (s32[4]{0:T(128)S(1)}, s32[12]{0:T(128)S(1)}, s32[]{:T(128)}, f32[2,3,8192]{2,1,0:T(4,128)S(1)}, f32[12,4,3,128]{3,1,2,0:T(4,128)S(1)}, /*index=5*/s32[12]{0:T(128)S(1)}, s32[12]{0:T(128)S(1)}, s32[12]{0:T(128)S(1)}, ...), branch_computations={%region_2.2_spmd, %region_3.5_spmd.clone} | conditional | flops 18620528 | bytes 496227 | solution.py:71
  90.4 10.3 %conditional.6 = (f32[1,4,5,128]{3,2,1,0:T(8,128)S(1)}) conditional(s32[]{:T(128)} %convert_element_type.49, () %tuple.138, (s32[4]{0:T(128)S(1)}, s32[12]{0:T(128)S(1)}, s32[]{:T(128)}, f32[2,3,8192]{2,1,0:T(4,128)S(1)}, f32[12,4,3,128]{3,1,2,0:T(4,128)S(1)}, /*index=5*/s32[12]{0:T(128)S(1)}, s32[12]{0:T(128)S(1)}, s32[12]{0:T(128)S(1)}, ...), branch_computations={%region_2.2_spmd, %region_3.5_spmd.clone} | conditional | flops 18620528 | bytes 496227 | solution.py:71
  102.0 10.3 %conditional.6 = (f32[1,4,5,128]{3,2,1,0:T(8,128)S(1)}) conditional(s32[]{:T(128)} %convert_element_type.49, () %tuple.138, (s32[4]{0:T(128)S(1)}, s32[12]{0:T(128)S(1)}, s32[]{:T(128)}, f32[2,3,8192]{2,1,0:T(4,128)S(1)}, f32[12,4,3,128]{3,1,2,0:T(4,128)S(1)}, /*index=5*/s32[12]{0:T(128)S(1)}, s32[12]{0:T(128)S(1)}, s32[12]{0:T(128)S(1)}, ...), branch_computations={%region_2.2_spmd, %region_3.5_spmd.clone} | conditional | flops 18620528 | bytes 496227 | solution.py:71
  113.7 10.3 %conditional.6 = (f32[1,4,5,128]{3,2,1,0:T(8,128)S(1)}) conditional(s32[]{:T(128)} %convert_element_type.49, () %tuple.138, (s32[4]{0:T(128)S(1)}, s32[12]{0:T(128)S(1)}, s32[]{:T(128)}, f32[2,3,8192]{2,1,0:T(4,128)S(1)}, f32[12,4,3,128]{3,1,2,0:T(4,128)S(1)}, /*index=5*/s32[12]{0:T(128)S(1)}, s32[12]{0:T(128)S(1)}, s32[12]{0:T(128)S(1)}, ...), branch_computations={%region_2.2_spmd, %region_3.5_spmd.clone} | conditional | flops 18620528 | bytes 496227 | solution.py:71
  125.3 10.3 %conditional.6 = (f32[1,4,5,128]{3,2,1,0:T(8,128)S(1)}) conditional(s32[]{:T(128)} %convert_element_type.49, () %tuple.138, (s32[4]{0:T(128)S(1)}, s32[12]{0:T(128)S(1)}, s32[]{:T(128)}, f32[2,3,8192]{2,1,0:T(4,128)S(1)}, f32[12,4,3,128]{3,1,2,0:T(4,128)S(1)}, /*index=5*/s32[12]{0:T(128)S(1)}, s32[12]{0:T(128)S(1)}, s32[12]{0:T(128)S(1)}, ...), branch_computations={%region_2.2_spmd, %region_3.5_spmd.clone} | conditional | flops 18620528 | bytes 496227 | solution.py:71
  136.9 10.3 %conditional.6 = (f32[1,4,5,128]{3,2,1,0:T(8,128)S(1)}) conditional(s32[]{:T(128)} %convert_element_type.49, () %tuple.138, (s32[4]{0:T(128)S(1)}, s32[12]{0:T(128)S(1)}, s32[]{:T(128)}, f32[2,3,8192]{2,1,0:T(4,128)S(1)}, f32[12,4,3,128]{3,1,2,0:T(4,128)S(1)}, /*index=5*/s32[12]{0:T(128)S(1)}, s32[12]{0:T(128)S(1)}, s32[12]{0:T(128)S(1)}, ...), branch_computations={%region_2.2_spmd, %region_3.5_spmd.clone} | conditional | flops 18620528 | bytes 496227 | solution.py:71
  148.6 10.3 %conditional.6 = (f32[1,4,5,128]{3,2,1,0:T(8,128)S(1)}) conditional(s32[]{:T(128)} %convert_element_type.49, () %tuple.138, (s32[4]{0:T(128)S(1)}, s32[12]{0:T(128)S(1)}, s32[]{:T(128)}, f32[2,3,8192]{2,1,0:T(4,128)S(1)}, f32[12,4,3,128]{3,1,2,0:T(4,128)S(1)}, /*index=5*/s32[12]{0:T(128)S(1)}, s32[12]{0:T(128)S(1)}, s32[12]{0:T(128)S(1)}, ...), branch_computations={%region_2.2_spmd, %region_3.5_spmd.clone} | conditional | flops 18620528 | bytes 496227 | solution.py:71
  160.2 10.3 %conditional.6 = (f32[1,4,5,128]{3,2,1,0:T(8,128)S(1)}) conditional(s32[]{:T(128)} %convert_element_type.49, () %tuple.138, (s32[4]{0:T(128)S(1)}, s32[12]{0:T(128)S(1)}, s32[]{:T(128)}, f32[2,3,8192]{2,1,0:T(4,128)S(1)}, f32[12,4,3,128]{3,1,2,0:T(4,128)S(1)}, /*index=5*/s32[12]{0:T(128)S(1)}, s32[12]{0:T(128)S(1)}, s32[12]{0:T(128)S(1)}, ...), branch_computations={%region_2.2_spmd, %region_3.5_spmd.clone} | conditional | flops 18620528 | bytes 496227 | solution.py:71
  171.9 10.3 %conditional.6 = (f32[1,4,5,128]{3,2,1,0:T(8,128)S(1)}) conditional(s32[]{:T(128)} %convert_element_type.49, () %tuple.138, (s32[4]{0:T(128)S(1)}, s32[12]{0:T(128)S(1)}, s32[]{:T(128)}, f32[2,3,8192]{2,1,0:T(4,128)S(1)}, f32[12,4,3,128]{3,1,2,0:T(4,128)S(1)}, /*index=5*/s32[12]{0:T(128)S(1)}, s32[12]{0:T(128)S(1)}, s32[12]{0:T(128)S(1)}, ...), branch_computations={%region_2.2_spmd, %region_3.5_spmd.clone} | conditional | flops 18620528 | bytes 496227 | solution.py:71
  195.2 10.3 %conditional.6 = (f32[1,4,5,128]{3,2,1,0:T(8,128)S(1)}) conditional(s32[]{:T(128)} %convert_element_type.49, () %tuple.138, (s32[4]{0:T(128)S(1)}, s32[12]{0:T(128)S(1)}, s32[]{:T(128)}, f32[2,3,8192]{2,1,0:T(4,128)S(1)}, f32[12,4,3,128]{3,1,2,0:T(4,128)S(1)}, /*index=5*/s32[12]{0:T(128)S(1)}, s32[12]{0:T(128)S(1)}, s32[12]{0:T(128)S(1)}, ...), branch_computations={%region_2.2_spmd, %region_3.5_spmd.clone} | conditional | flops 18620528 | bytes 496227 | solution.py:71
  217.4 34.0 %all-reduce.6 = (f32[3,4]{1,0:T(4,128)S(1)}, f32[4,4]{0,1:T(4,128)S(1)}) all-reduce(f32[3,4]{1,0:T(4,128)S(1)} %convolution_bitcast_fusion.6, f32[4,4]{0,1:T(4,128)S(1)} %convolution_bitcast_fusion.7), channel_id=1, replica_groups=mesh['line'=32,'seg'=16] {'seg'}, use_global_device_ids=true, to_apply=%region_10.12 | all-reduce | flops 28 | bytes 224 | tf_op jit(solution)/shard_map/psum | solution.py:158
  254.3 16.7 %convolution_add_fusion = f32[3,32768]{1,0:T(4,128)S(1)} fusion(f32[3]{0:T(128)S(1)} %slice_reduce_fusion.3, f32[3,4]{1,0:T(4,128)S(1)} %convolution_bitcast_fusion.5, f32[1,1,3,32768]{2,3,1,0:T(8,128)} %copy.18), kind=kOutput, calls=%fused_computation.60 | convolution fusion | flops 3637248 | bytes 786492 | tf_op jit(solution)/shard_map/dot_general | solution.py:123
  278.9 98.2 %all-reduce.4 = (f32[]{:T(128)}, f32[]{:T(128)}) all-reduce(f32[]{:T(128)} %get-tuple-element.356, f32[]{:T(128)} %get-tuple-element.355), channel_id=1, replica_groups=mesh['line'=32,'seg'=16] {'line','seg'}, use_global_device_ids=true, to_apply=%region_12.15 | all-reduce | flops 2 | bytes 16 | tf_op jit(solution)/shard_map/psum | solution.py:159
  378.5 140.6 %while.29 = (s32[]{:T(128)}, f32[12,4,5,128]{3,2,1,0:T(8,128)S(1)}, s32[12,4]{1,0:T(8,128)S(1)}, f32[2,3,8192]{2,1,0:T(4,128)S(1)}, f32[12,4,3,128]{3,1,2,0:T(4,...) while((s32[]{:T(128)}, f32[12,4,5,128]{3,2,1,0:T(8,128)S(1)}, ...), condition=%wide.region_21.24_spmd.clone, body=%wide.region_15.23_spmd.clone.sunk | while | flops 18620552 | bytes 529402 | solution.py:73
  379.9 10.4 %conditional.7 = (f32[1,4,5,128]{3,2,1,0:T(8,128)S(1)}) conditional(s32[]{:T(128)} %convert_element_type.50, () %tuple.142, (s32[4]{0:T(128)S(1)}, s32[12]{0:T(128)S(1)}, s32[]{:T(128)}, f32[2,3,8192]{2,1,0:T(4,128)S(1)}, f32[12,4,3,128]{3,1,2,0:T(4,128)S(1)}, /*index=5*/f32[]{:T(128)}, s32[12]{0:T(128)S(1)}, s32[12]{0:T(128)S(1)}, ...), branch_computations={%region_17.19_spmd, %region_18.22_spmd.clone} | conditional | flops 18620530 | bytes 496251 | solution.py:71
  391.6 10.4 %conditional.7 = (f32[1,4,5,128]{3,2,1,0:T(8,128)S(1)}) conditional(s32[]{:T(128)} %convert_element_type.50, () %tuple.142, (s32[4]{0:T(128)S(1)}, s32[12]{0:T(128)S(1)}, s32[]{:T(128)}, f32[2,3,8192]{2,1,0:T(4,128)S(1)}, f32[12,4,3,128]{3,1,2,0:T(4,128)S(1)}, /*index=5*/f32[]{:T(128)}, s32[12]{0:T(128)S(1)}, s32[12]{0:T(128)S(1)}, ...), branch_computations={%region_17.19_spmd, %region_18.22_spmd.clone} | conditional | flops 18620530 | bytes 496251 | solution.py:71
  403.3 10.4 %conditional.7 = (f32[1,4,5,128]{3,2,1,0:T(8,128)S(1)}) conditional(s32[]{:T(128)} %convert_element_type.50, () %tuple.142, (s32[4]{0:T(128)S(1)}, s32[12]{0:T(128)S(1)}, s32[]{:T(128)}, f32[2,3,8192]{2,1,0:T(4,128)S(1)}, f32[12,4,3,128]{3,1,2,0:T(4,128)S(1)}, /*index=5*/f32[]{:T(128)}, s32[12]{0:T(128)S(1)}, s32[12]{0:T(128)S(1)}, ...), branch_computations={%region_17.19_spmd, %region_18.22_spmd.clone} | conditional | flops 18620530 | bytes 496251 | solution.py:71
  415.0 10.4 %conditional.7 = (f32[1,4,5,128]{3,2,1,0:T(8,128)S(1)}) conditional(s32[]{:T(128)} %convert_element_type.50, () %tuple.142, (s32[4]{0:T(128)S(1)}, s32[12]{0:T(128)S(1)}, s32[]{:T(128)}, f32[2,3,8192]{2,1,0:T(4,128)S(1)}, f32[12,4,3,128]{3,1,2,0:T(4,128)S(1)}, /*index=5*/f32[]{:T(128)}, s32[12]{0:T(128)S(1)}, s32[12]{0:T(128)S(1)}, ...), branch_computations={%region_17.19_spmd, %region_18.22_spmd.clone} | conditional | flops 18620530 | bytes 496251 | solution.py:71
  426.7 10.4 %conditional.7 = (f32[1,4,5,128]{3,2,1,0:T(8,128)S(1)}) conditional(s32[]{:T(128)} %convert_element_type.50, () %tuple.142, (s32[4]{0:T(128)S(1)}, s32[12]{0:T(128)S(1)}, s32[]{:T(128)}, f32[2,3,8192]{2,1,0:T(4,128)S(1)}, f32[12,4,3,128]{3,1,2,0:T(4,128)S(1)}, /*index=5*/f32[]{:T(128)}, s32[12]{0:T(128)S(1)}, s32[12]{0:T(128)S(1)}, ...), branch_computations={%region_17.19_spmd, %region_18.22_spmd.clone} | conditional | flops 18620530 | bytes 496251 | solution.py:71
  438.4 10.4 %conditional.7 = (f32[1,4,5,128]{3,2,1,0:T(8,128)S(1)}) conditional(s32[]{:T(128)} %convert_element_type.50, () %tuple.142, (s32[4]{0:T(128)S(1)}, s32[12]{0:T(128)S(1)}, s32[]{:T(128)}, f32[2,3,8192]{2,1,0:T(4,128)S(1)}, f32[12,4,3,128]{3,1,2,0:T(4,128)S(1)}, /*index=5*/f32[]{:T(128)}, s32[12]{0:T(128)S(1)}, s32[12]{0:T(128)S(1)}, ...), branch_computations={%region_17.19_spmd, %region_18.22_spmd.clone} | conditional | flops 18620530 | bytes 496251 | solution.py:71
  450.1 10.4 %conditional.7 = (f32[1,4,5,128]{3,2,1,0:T(8,128)S(1)}) conditional(s32[]{:T(128)} %convert_element_type.50, () %tuple.142, (s32[4]{0:T(128)S(1)}, s32[12]{0:T(128)S(1)}, s32[]{:T(128)}, f32[2,3,8192]{2,1,0:T(4,128)S(1)}, f32[12,4,3,128]{3,1,2,0:T(4,128)S(1)}, /*index=5*/f32[]{:T(128)}, s32[12]{0:T(128)S(1)}, s32[12]{0:T(128)S(1)}, ...), branch_computations={%region_17.19_spmd, %region_18.22_spmd.clone} | conditional | flops 18620530 | bytes 496251 | solution.py:71
  461.8 10.4 %conditional.7 = (f32[1,4,5,128]{3,2,1,0:T(8,128)S(1)}) conditional(s32[]{:T(128)} %convert_element_type.50, () %tuple.142, (s32[4]{0:T(128)S(1)}, s32[12]{0:T(128)S(1)}, s32[]{:T(128)}, f32[2,3,8192]{2,1,0:T(4,128)S(1)}, f32[12,4,3,128]{3,1,2,0:T(4,128)S(1)}, /*index=5*/f32[]{:T(128)}, s32[12]{0:T(128)S(1)}, s32[12]{0:T(128)S(1)}, ...), branch_computations={%region_17.19_spmd, %region_18.22_spmd.clone} | conditional | flops 18620530 | bytes 496251 | solution.py:71
  473.6 10.4 %conditional.7 = (f32[1,4,5,128]{3,2,1,0:T(8,128)S(1)}) conditional(s32[]{:T(128)} %convert_element_type.50, () %tuple.142, (s32[4]{0:T(128)S(1)}, s32[12]{0:T(128)S(1)}, s32[]{:T(128)}, f32[2,3,8192]{2,1,0:T(4,128)S(1)}, f32[12,4,3,128]{3,1,2,0:T(4,128)S(1)}, /*index=5*/f32[]{:T(128)}, s32[12]{0:T(128)S(1)}, s32[12]{0:T(128)S(1)}, ...), branch_computations={%region_17.19_spmd, %region_18.22_spmd.clone} | conditional | flops 18620530 | bytes 496251 | solution.py:71
  485.3 10.4 %conditional.7 = (f32[1,4,5,128]{3,2,1,0:T(8,128)S(1)}) conditional(s32[]{:T(128)} %convert_element_type.50, () %tuple.142, (s32[4]{0:T(128)S(1)}, s32[12]{0:T(128)S(1)}, s32[]{:T(128)}, f32[2,3,8192]{2,1,0:T(4,128)S(1)}, f32[12,4,3,128]{3,1,2,0:T(4,128)S(1)}, /*index=5*/f32[]{:T(128)}, s32[12]{0:T(128)S(1)}, s32[12]{0:T(128)S(1)}, ...), branch_computations={%region_17.19_spmd, %region_18.22_spmd.clone} | conditional | flops 18620530 | bytes 496251 | solution.py:71
  497.0 10.4 %conditional.7 = (f32[1,4,5,128]{3,2,1,0:T(8,128)S(1)}) conditional(s32[]{:T(128)} %convert_element_type.50, () %tuple.142, (s32[4]{0:T(128)S(1)}, s32[12]{0:T(128)S(1)}, s32[]{:T(128)}, f32[2,3,8192]{2,1,0:T(4,128)S(1)}, f32[12,4,3,128]{3,1,2,0:T(4,128)S(1)}, /*index=5*/f32[]{:T(128)}, s32[12]{0:T(128)S(1)}, s32[12]{0:T(128)S(1)}, ...), branch_computations={%region_17.19_spmd, %region_18.22_spmd.clone} | conditional | flops 18620530 | bytes 496251 | solution.py:71
  508.7 10.4 %conditional.7 = (f32[1,4,5,128]{3,2,1,0:T(8,128)S(1)}) conditional(s32[]{:T(128)} %convert_element_type.50, () %tuple.142, (s32[4]{0:T(128)S(1)}, s32[12]{0:T(128)S(1)}, s32[]{:T(128)}, f32[2,3,8192]{2,1,0:T(4,128)S(1)}, f32[12,4,3,128]{3,1,2,0:T(4,128)S(1)}, /*index=5*/f32[]{:T(128)}, s32[12]{0:T(128)S(1)}, s32[12]{0:T(128)S(1)}, ...), branch_computations={%region_17.19_spmd, %region_18.22_spmd.clone} | conditional | flops 18620530 | bytes 496251 | solution.py:71
  530.3 101.3 %all-reduce.3 = (f32[]{:T(128)}, f32[]{:T(128)}) all-reduce(f32[]{:T(128)} %get-tuple-element.354, f32[]{:T(128)} %get-tuple-element.353), channel_id=1, replica_groups=mesh['line'=32,'seg'=16] {'line','seg'}, use_global_device_ids=true, to_apply=%region_25.28 | all-reduce | flops 2 | bytes 16 | tf_op jit(solution)/shard_map/psum | solution.py:159
  633.5 29.0 %all-reduce.5 = (f32[4,4]{0,1:T(4,128)S(1)}, f32[3,4]{1,0:T(4,128)S(1)}) all-reduce(f32[4,4]{0,1:T(4,128)S(1)} %convolution_bitcast_fusion.4, f32[3,4]{1,0:T(4,128)S(1)} %convolution_bitcast_fusion.3), channel_id=1, replica_groups=mesh['line'=32,'seg'=16] {'seg'}, use_global_device_ids=true, to_apply=%region_22.25 | all-reduce | flops 28 | bytes 224 | tf_op jit(solution)/shard_map/psum | solution.py:158
  (965 shorter events, 414.3 us)
Async XLA Ops:
  0.6 43.6 %copy-start = (s32[1,1,2,24]{3,2,1,0:T(2,128)S(1)}, s32[1,1,2,24]{3,2,1,0:T(2,128)}, u32[]{:S(2)}) copy-start(s32[1,1,2,24]{3,2,1,0:T(2,128)} %param.17) | copy-start | bytes 580
  36.6 29.1 %collective-permute-start.3 = (f32[3,3072]{1,0:T(4,128)S(1)}, f32[3,3072]{1,0:T(4,128)S(1)}, u32[]{:S(2)}, u32[]{:S(2)}) collective-permute-start(f32[3,3072]{1,0:T(4,128)S(1)} %get-tuple-element.436), channel_id=1, source_target_pairs={{0,16},{16,32},{32,48},{48,64},{64,80},{80,96},{96,112},{112,128},... | collective-permute-start | bytes 110600 | tf_op jit(solution)/shard_map/ppermute | solution.py:21
  38.5 27.2 %collective-permute-start.2 = (f32[3,3072]{1,0:T(4,128)S(1)}, f32[3,3072]{1,0:T(4,128)S(1)}, u32[]{:S(2)}, u32[]{:S(2)}) collective-permute-start(f32[3,3072]{1,0:T(4,128)S(1)} %get-tuple-element.435), channel_id=1, source_target_pairs={{16,0},{32,16},{48,32},{64,48},{80,64},{96,80},{112,96},{128,112},... | collective-permute-start | bytes 110600 | tf_op jit(solution)/shard_map/ppermute | solution.py:21
  44.3 21.3 %collective-permute-start = (f32[24]{0:T(128)S(1)}, f32[24]{0:T(128)S(1)}, u32[]{:S(2)}, u32[]{:S(2)}) collective-permute-start(f32[24]{0:T(128)S(1)} %get-tuple-element.439), channel_id=1, source_target_pairs={{16,0},{32,16},{48,32},{64,48},{80,64},{96,80},{112,96},{128,112},... | collective-permute-start | bytes 296 | tf_op jit(solution)/shard_map/ppermute | solution.py:21
  46.2 19.4 %collective-permute-start.1 = (f32[24]{0:T(128)S(1)}, f32[24]{0:T(128)S(1)}, u32[]{:S(2)}, u32[]{:S(2)}) collective-permute-start(f32[24]{0:T(128)S(1)} %get-tuple-element.440), channel_id=1, source_target_pairs={{0,16},{16,32},{32,48},{48,64},{64,80},{80,96},{96,112},{112,128},... | collective-permute-start | bytes 296 | tf_op jit(solution)/shard_map/ppermute | solution.py:21
  205.6 8.0 %collective-permute-start.4 = (f32[5,3072]{1,0:T(8,128)S(1)}, f32[5,3072]{1,0:T(8,128)S(1)}, u32[]{:S(2)}, u32[]{:S(2)}) collective-permute-start(f32[5,3072]{1,0:T(8,128)S(1)} %bitcast.309), channel_id=1, source_target_pairs={{0,16},{16,32},{32,48},{48,64},{64,80},{80,96},{96,112},{112,128},... | collective-permute-start | bytes 184328 | tf_op jit(solution)/shard_map/ppermute | solution.py:21
  207.5 8.0 %collective-permute-start.5 = (f32[5,3072]{1,0:T(8,128)S(1)}, f32[5,3072]{1,0:T(8,128)S(1)}, u32[]{:S(2)}, u32[]{:S(2)}) collective-permute-start(f32[5,3072]{1,0:T(8,128)S(1)} %bitcast.311), channel_id=1, source_target_pairs={{16,0},{32,16},{48,32},{64,48},{80,64},{96,80},{112,96},{128,112},... | collective-permute-start | bytes 184328 | tf_op jit(solution)/shard_map/ppermute | solution.py:21
  271.1 107.3 %collective-permute-start.7 = (f32[3,3072]{1,0:T(4,128)S(1)}, f32[3,3072]{1,0:T(4,128)S(1)}, u32[]{:S(2)}, u32[]{:S(2)}) collective-permute-start(f32[3,3072]{1,0:T(4,128)S(1)} %get-tuple-element.434), channel_id=1, source_target_pairs={{0,16},{16,32},{32,48},{48,64},{64,80},{80,96},{96,112},{112,128},... | collective-permute-start | bytes 110600 | tf_op jit(solution)/shard_map/ppermute | solution.py:21
  273.0 105.4 %collective-permute-start.6 = (f32[3,3072]{1,0:T(4,128)S(1)}, f32[3,3072]{1,0:T(4,128)S(1)}, u32[]{:S(2)}, u32[]{:S(2)}) collective-permute-start(f32[3,3072]{1,0:T(4,128)S(1)} %get-tuple-element.433), channel_id=1, source_target_pairs={{16,0},{32,16},{48,32},{64,48},{80,64},{96,80},{112,96},{128,112},... | collective-permute-start | bytes 110600 | tf_op jit(solution)/shard_map/ppermute | solution.py:21
  519.2 8.0 %collective-permute-start.8 = (f32[5,3072]{1,0:T(8,128)S(1)}, f32[5,3072]{1,0:T(8,128)S(1)}, u32[]{:S(2)}, u32[]{:S(2)}) collective-permute-start(f32[5,3072]{1,0:T(8,128)S(1)} %bitcast.310), channel_id=1, source_target_pairs={{0,16},{16,32},{32,48},{48,64},{64,80},{80,96},{96,112},{112,128},... | collective-permute-start | bytes 184328 | tf_op jit(solution)/shard_map/ppermute | solution.py:21
  521.1 8.0 %collective-permute-start.9 = (f32[5,3072]{1,0:T(8,128)S(1)}, f32[5,3072]{1,0:T(8,128)S(1)}, u32[]{:S(2)}, u32[]{:S(2)}) collective-permute-start(f32[5,3072]{1,0:T(8,128)S(1)} %bitcast.312), channel_id=1, source_target_pairs={{16,0},{32,16},{48,32},{64,48},{80,64},{96,80},{112,96},{128,112},... | collective-permute-start | bytes 184328 | tf_op jit(solution)/shard_map/ppermute | solution.py:21
where the time goes:
time: 670 us; the launch traced here: 668 us
  blocking collectives  262 us (39%)
  local copies, waits for them, and re-layouts  170 us (25%)
  matrix products  70.6 us (11%)
  other arithmetic  60.7 us (9%)
  loops' own time  59.3 us (9%)
  starting transfers between devices  35 us (5%)
    psum x2, blocking collectives, on_device(): energy_sum, share_sum = lax.psum((energy_part, share_part), ('line', 'seg'))  199 us
    gather x288, local copies, waits for them, and re-layouts  118 us
    psum x2, blocking collectives, on_device(): gram_sum, cross_sum = lax.psum((gram_matrix, cross_matrix), 'seg')  63 us
    another operation x24, loops' own time, one_turn(): return lax.cond(jnp.any(turn_cells >= 0), compute, skipped, 0)  43.1 us
    ppermute x10, starting transfers between devices, from_behind(): lax.ppermute(value, axis, [(source, source + steps) for source in range(i...  35 us
    dot_general x24, matrix products, match_block(): lax.dot_general(target, posterior, (((1,), (1,)), ((), ())), precision=la...  33.6 us
    dot_general x2, matrix products, on_device(): jnp.dot(linear_part, own_points, precision=lax.Precision.HIGHEST, preferr...  33.5 us
    gather x2, local copies, waits for them, and re-layouts, on_device(): jnp.take(own_points, safe_rows.reshape(-1), axis=1)  23 us
  transfers between devices with their start and end apart: 10, of which 4 were waited for; matrix products, arithmetic and copies ran while one was open for 3% of the time, Pallas kernels for 0%

commit v1 on v0

--- a/solution.py
+++ b/solution.py
@@ -156,7 +156,7 @@
         energy_part = jnp.sum(energy_all)
         share_part = jnp.sum(share_all)
         gram_sum, cross_sum = lax.psum((gram_matrix, cross_matrix), "seg")
-        energy_sum, share_sum = lax.psum((energy_part, share_part), ("line", "seg"))
+        energy_sum, share_sum = lax.psum(lax.psum((energy_part, share_part), "line"), "seg")
         pose_column = solve_pose(gram_sum, cross_sum, pose_column)
         spread = (energy_sum + PRIOR_TOP) / (3.0 * share_sum + PRIOR_BOTTOM)
     return (result[None, None], pose_column[:, None], spread.reshape(1))

time: 670 us -> 590 us (0.88)
  the two profiles are of different devices: /device:TPU:2 before, /device:TPU:32 now
where the time goes in v1:
time: 590 us; the launch traced here: 587 us
  blocking collectives  260 us (44%)
  starting transfers between devices  82.8 us (14%)
  local copies, waits for them, and re-layouts  70.5 us (12%)
  waiting for transfers between devices  64 us (11%)
  matrix products  45.4 us (8%)
  other arithmetic  32.1 us (5%)
  loops' own time  27.5 us (5%)
    psum x2, blocking collectives, on_device(): lax.psum((energy_part, share_part), 'line')  180 us
    ppermute x10, starting transfers between devices, from_behind(): lax.ppermute(value, axis, [(source, source + steps) for source in range(i...  82.8 us
    psum x2, blocking collectives, on_device(): gram_sum, cross_sum = lax.psum((gram_matrix, cross_matrix), 'seg')  80.3 us
    ppermute x10, waiting for transfers between devices, from_behind(): lax.ppermute(value, axis, [(source, source + steps) for source in range(i...  64 us
    dot_general x2, matrix products, on_device(): jnp.dot(linear_part, own_points, precision=lax.Precision.HIGHEST, preferr...  33.5 us
    gather x72, local copies, waits for them, and re-layouts  29.4 us
    gather x2, local copies, waits for them, and re-layouts, on_device(): jnp.take(own_points, safe_rows.reshape(-1), axis=1)  23 us
    another operation x2, loops' own time, match_all(): output = lax.map(one_turn, (grouped, grouped_cells, sides))  16.2 us
  transfers between devices with their start and end apart: 10, of which 3 were waited for; matrix products, arithmetic and copies ran while one was open for 3% of the time, Pallas kernels for 0%

profile of v1, /device:TPU:32, one launch (start us, length us, event | category | flops | bytes accessed | tf_op | source)
XLA Modules:
  0.0 587.3 jit_solution(1382154417692677528)
XLA Ops:
  3.6 9.4 %copy.18 = f32[1,1,3,32768]{2,3,1,0:T(8,128)} copy(f32[1,1,3,32768]{3,1,2,0:T(1,128)} %param.15) | data formatting | bytes 786432 | tf_op args[0]
  13.1 21.8 %gather_fusion = f32[6144,3]{1,0:T(8,128)S(1)} fusion(f32[3,32768]{0,1:T(8,128)} %bitcast.285, s32[6144]{0:T(1024)S(1)} %broadcast_clamp_fusion), kind=kCustom, calls=%fused_computation | custom fusion | bytes 172032 | tf_op jit(solution)/shard_map/jit(_take)/gather | solution.py:112
  36.5 1.7 collective-permute-start.3
  40.9 5.0 collective-permute-start.1
  46.0 16.7 %convolution_add_fusion.1 = f32[3,32768]{1,0:T(4,128)S(1)} fusion(f32[3,3]{1,0:T(4,128)S(1)} %reshape.263, f32[3]{0:T(128)S(1)} %get-tuple-element.446, f32[1,1,3,32768]{2,3,1,0:T(8,128)} %copy.18), kind=kOutput, calls=%fused_computation.61 | convolution fusion | flops 3637248 | bytes 786480 | tf_op jit(solution)/shard_map/dot_general | solution.py:123
  63.1 47.2 %while.28 = (s32[]{:T(128)}, f32[12,4,5,128]{3,2,1,0:T(8,128)S(1)}, s32[12,4]{1,0:T(8,128)S(1)}, f32[2,3,8192]{2,1,0:T(4,128)S(1)}, f32[12,4,3,128]{3,1,2,0:T(4,128)S(1)}, /*index=5*/s32[]{:T(128)}, s32[]{:T(128)}, s32[]{:T(128)}) while((s32[]{:T(128)}, f32[12,4,5,128]{3,2,1,0:T(8,128)S(1)}, s32[12,4]{1,0:T(8,128)S(1)}, ...), condition=%wide.region_6.7_spmd.clone, body=%wide.region_0.6_spmd.clone.sunk | while | flops 18620548 | bytes 529362 | solution.py:73
  64.4 10.3 %conditional.6 = (f32[1,4,5,128]{3,2,1,0:T(8,128)S(1)}) conditional(s32[]{:T(128)} %convert_element_type.49, () %tuple.138, (s32[4]{0:T(128)S(1)}, s32[12]{0:T(128)S(1)}, s32[]{:T(128)}, f32[2,3,8192]{2,1,0:T(4,128)S(1)}, f32[12,4,3,128]{3,1,2,0:T(4,128)S(1)}, /*index=5*/s32[12]{0:T(128)S(1)}, s32[12]{0:T(128)S(1)}, s32[12]{0:T(128)S(1)}, ...), branch_computations={%region_2.2_spmd, %region_3.5_spmd.clone} | conditional | flops 18620528 | bytes 496227 | solution.py:71
  66.9 4.9 while.26
  72.5 1.4 convolution_bitcast_fusion
  76.1 10.3 %conditional.6 = (f32[1,4,5,128]{3,2,1,0:T(8,128)S(1)}) conditional(s32[]{:T(128)} %convert_element_type.49, () %tuple.138, (s32[4]{0:T(128)S(1)}, s32[12]{0:T(128)S(1)}, s32[]{:T(128)}, f32[2,3,8192]{2,1,0:T(4,128)S(1)}, f32[12,4,3,128]{3,1,2,0:T(4,128)S(1)}, /*index=5*/s32[12]{0:T(128)S(1)}, s32[12]{0:T(128)S(1)}, s32[12]{0:T(128)S(1)}, ...), branch_computations={%region_2.2_spmd, %region_3.5_spmd.clone} | conditional | flops 18620528 | bytes 496227 | solution.py:71
  78.6 4.9 while.26
  87.7 10.3 %conditional.6 = (f32[1,4,5,128]{3,2,1,0:T(8,128)S(1)}) conditional(s32[]{:T(128)} %convert_element_type.49, () %tuple.138, (s32[4]{0:T(128)S(1)}, s32[12]{0:T(128)S(1)}, s32[]{:T(128)}, f32[2,3,8192]{2,1,0:T(4,128)S(1)}, f32[12,4,3,128]{3,1,2,0:T(4,128)S(1)}, /*index=5*/s32[12]{0:T(128)S(1)}, s32[12]{0:T(128)S(1)}, s32[12]{0:T(128)S(1)}, ...), branch_computations={%region_2.2_spmd, %region_3.5_spmd.clone} | conditional | flops 18620528 | bytes 496227 | solution.py:71
  90.2 4.9 while.26
  110.4 34.5 %collective-permute-start.4 = (f32[5,3072]{1,0:T(8,128)S(1)}, f32[5,3072]{1,0:T(8,128)S(1)}, u32[]{:S(2)}, u32[]{:S(2)}) collective-permute-start(f32[5,3072]{1,0:T(8,128)S(1)} %bitcast.309), channel_id=1, source_target_pairs={{0,16},{16,32},{32,48},{48,64},{64,80},{80,96},{96,112},{112,128},... | collective-permute-start | bytes 184328 | tf_op jit(solution)/shard_map/ppermute | solution.py:21
  146.3 32.6 %collective-permute-done.5 = f32[5,3072]{1,0:T(8,128)S(1)} collective-permute-done((f32[5,3072]{1,0:T(8,128)S(1)}, f32[5,3072]{1,0:T(8,128)S(1)}, u32[]{:S(2)}, u32[]{:S(2)}) %collective-permute-start.5) | collective-permute-done | bytes 61472 | tf_op jit(solution)/shard_map/ppermute | solution.py:21
  180.8 89.2 %all-reduce.4 = (f32[]{:T(128)}, f32[]{:T(128)}) all-reduce(f32[]{:T(128)} %get-tuple-element.356, f32[]{:T(128)} %get-tuple-element.355), channel_id=1, replica_groups=mesh['line'=32,'seg'=16] {'line'}, use_global_device_ids=true, to_apply=%region_12.15 | all-reduce | flops 2 | bytes 16 | tf_op jit(solution)/shard_map/psum | solution.py:159
  269.9 43.9 %all-reduce.6 = (f32[3,4]{1,0:T(4,128)S(1)}, f32[4,4]{0,1:T(4,128)S(1)}, f32[]{:T(128)}, f32[]{:T(128)}) all-reduce(f32[3,4]{1,0:T(4,128)S(1)} %convolution_bitcast_fusion.6, f32[4,4]{0,1:T(4,128)S(1)} %convolution_bitcast_fusion.7, f32[]{:T(128)} %get-tuple-element.397, ...), channel_id=1, replica_groups=mesh['line'=32,'seg'=16] {'seg'}, use_global_device_ids=true, to_apply=%region_10.12 | all-reduce | flops 30 | bytes 240 | tf_op jit(solution)/shard_map/psum | solution.py:158
  316.8 16.7 %convolution_add_fusion = f32[3,32768]{1,0:T(4,128)S(1)} fusion(f32[3]{0:T(128)S(1)} %slice_reduce_fusion.3, f32[3,4]{1,0:T(4,128)S(1)} %convolution_bitcast_fusion.5, f32[1,1,3,32768]{2,3,1,0:T(8,128)} %copy.18), kind=kOutput, calls=%fused_computation.60 | convolution fusion | flops 3637248 | bytes 786492 | tf_op jit(solution)/shard_map/dot_general | solution.py:123
  338.1 47.4 %while.29 = (s32[]{:T(128)}, f32[12,4,5,128]{3,2,1,0:T(8,128)S(1)}, s32[12,4]{1,0:T(8,128)S(1)}, f32[2,3,8192]{2,1,0:T(4,128)S(1)}, f32[12,4,3,128]{3,1,2,0:T(4,...) while((s32[]{:T(128)}, f32[12,4,5,128]{3,2,1,0:T(8,128)S(1)}, ...), condition=%wide.region_23.26_spmd.clone, body=%wide.region_17.25_spmd.clone.sunk | while | flops 18620552 | bytes 529402 | solution.py:73
  339.4 10.4 %conditional.7 = (f32[1,4,5,128]{3,2,1,0:T(8,128)S(1)}) conditional(s32[]{:T(128)} %convert_element_type.50, () %tuple.142, (s32[4]{0:T(128)S(1)}, s32[12]{0:T(128)S(1)}, s32[]{:T(128)}, f32[2,3,8192]{2,1,0:T(4,128)S(1)}, f32[12,4,3,128]{3,1,2,0:T(4,128)S(1)}, /*index=5*/f32[]{:T(128)}, s32[12]{0:T(128)S(1)}, s32[12]{0:T(128)S(1)}, ...), branch_computations={%region_19.21_spmd, %region_20.24_spmd.clone} | conditional | flops 18620530 | bytes 496251 | solution.py:71
  341.9 4.9 while.27
  347.5 1.4 convolution_bitcast_fusion.1
  351.1 10.4 %conditional.7 = (f32[1,4,5,128]{3,2,1,0:T(8,128)S(1)}) conditional(s32[]{:T(128)} %convert_element_type.50, () %tuple.142, (s32[4]{0:T(128)S(1)}, s32[12]{0:T(128)S(1)}, s32[]{:T(128)}, f32[2,3,8192]{2,1,0:T(4,128)S(1)}, f32[12,4,3,128]{3,1,2,0:T(4,128)S(1)}, /*index=5*/f32[]{:T(128)}, s32[12]{0:T(128)S(1)}, s32[12]{0:T(128)S(1)}, ...), branch_computations={%region_19.21_spmd, %region_20.24_spmd.clone} | conditional | flops 18620530 | bytes 496251 | solution.py:71
  353.6 4.9 while.27
  359.2 1.4 convolution_bitcast_fusion.1
  362.8 10.4 %conditional.7 = (f32[1,4,5,128]{3,2,1,0:T(8,128)S(1)}) conditional(s32[]{:T(128)} %convert_element_type.50, () %tuple.142, (s32[4]{0:T(128)S(1)}, s32[12]{0:T(128)S(1)}, s32[]{:T(128)}, f32[2,3,8192]{2,1,0:T(4,128)S(1)}, f32[12,4,3,128]{3,1,2,0:T(4,128)S(1)}, /*index=5*/f32[]{:T(128)}, s32[12]{0:T(128)S(1)}, s32[12]{0:T(128)S(1)}, ...), branch_computations={%region_19.21_spmd, %region_20.24_spmd.clone} | conditional | flops 18620530 | bytes 496251 | solution.py:71
  365.3 4.9 while.27
  370.9 1.4 convolution_bitcast_fusion.1
  385.6 33.8 %collective-permute-start.8 = (f32[5,3072]{1,0:T(8,128)S(1)}, f32[5,3072]{1,0:T(8,128)S(1)}, u32[]{:S(2)}, u32[]{:S(2)}) collective-permute-start(f32[5,3072]{1,0:T(8,128)S(1)} %bitcast.311), channel_id=1, source_target_pairs={{0,16},{16,32},{32,48},{48,64},{64,80},{80,96},{96,112},{112,128},... | collective-permute-start | bytes 184328 | tf_op jit(solution)/shard_map/ppermute | solution.py:21
  420.7 31.1 %collective-permute-done.9 = f32[5,3072]{1,0:T(8,128)S(1)} collective-permute-done((f32[5,3072]{1,0:T(8,128)S(1)}, f32[5,3072]{1,0:T(8,128)S(1)}, u32[]{:S(2)}, u32[]{:S(2)}) %collective-permute-start.9) | collective-permute-done | bytes 61472 | tf_op jit(solution)/shard_map/ppermute | solution.py:21
  453.5 90.7 %all-reduce.3 = (f32[]{:T(128)}, f32[]{:T(128)}) all-reduce(f32[]{:T(128)} %get-tuple-element.354, f32[]{:T(128)} %get-tuple-element.353), channel_id=1, replica_groups=mesh['line'=32,'seg'=16] {'line'}, use_global_device_ids=true, to_apply=%region_27.30 | all-reduce | flops 2 | bytes 16 | tf_op jit(solution)/shard_map/psum | solution.py:159
  544.3 36.4 %all-reduce.5 = (f32[4,4]{0,1:T(4,128)S(1)}, f32[3,4]{1,0:T(4,128)S(1)}, f32[]{:T(128)}, f32[]{:T(128)}) all-reduce(f32[4,4]{0,1:T(4,128)S(1)} %convolution_bitcast_fusion.4, f32[3,4]{1,0:T(4,128)S(1)} %convolution_bitcast_fusion.3, f32[]{:T(128)} %get-tuple-element.395, ...), channel_id=1, replica_groups=mesh['line'=32,'seg'=16] {'seg'}, use_global_device_ids=true, to_apply=%region_24.27 | all-reduce | flops 30 | bytes 240 | tf_op jit(solution)/shard_map/psum | solution.py:158
  (425 shorter events, 86.1 us)
Async XLA Ops:
  0.6 39.0 %copy-start = (s32[1,1,2,24]{3,2,1,0:T(2,128)S(1)}, s32[1,1,2,24]{3,2,1,0:T(2,128)}, u32[]{:S(2)}) copy-start(s32[1,1,2,24]{3,2,1,0:T(2,128)} %param.17) | copy-start | bytes 580
  36.5 26.5 %collective-permute-start.3 = (f32[3,3072]{1,0:T(4,128)S(1)}, f32[3,3072]{1,0:T(4,128)S(1)}, u32[]{:S(2)}, u32[]{:S(2)}) collective-permute-start(f32[3,3072]{1,0:T(4,128)S(1)} %get-tuple-element.440), channel_id=1, source_target_pairs={{0,16},{16,32},{32,48},{48,64},{64,80},{80,96},{96,112},{112,128},... | collective-permute-start | bytes 110600 | tf_op jit(solution)/shard_map/ppermute | solution.py:21
  38.3 24.7 %collective-permute-start.2 = (f32[3,3072]{1,0:T(4,128)S(1)}, f32[3,3072]{1,0:T(4,128)S(1)}, u32[]{:S(2)}, u32[]{:S(2)}) collective-permute-start(f32[3,3072]{1,0:T(4,128)S(1)} %get-tuple-element.439), channel_id=1, source_target_pairs={{16,0},{32,16},{48,32},{64,48},{80,64},{96,80},{112,96},{128,112},... | collective-permute-start | bytes 110600 | tf_op jit(solution)/shard_map/ppermute | solution.py:21
  39.6 23.3 %collective-permute-start = (f32[24]{0:T(128)S(1)}, f32[24]{0:T(128)S(1)}, u32[]{:S(2)}, u32[]{:S(2)}) collective-permute-start(f32[24]{0:T(128)S(1)} %get-tuple-element.443), channel_id=1, source_target_pairs={{16,0},{32,16},{48,32},{64,48},{80,64},{96,80},{112,96},{128,112},... | collective-permute-start | bytes 296 | tf_op jit(solution)/shard_map/ppermute | solution.py:21
  40.9 22.0 %collective-permute-start.1 = (f32[24]{0:T(128)S(1)}, f32[24]{0:T(128)S(1)}, u32[]{:S(2)}, u32[]{:S(2)}) collective-permute-start(f32[24]{0:T(128)S(1)} %get-tuple-element.444), channel_id=1, source_target_pairs={{0,16},{16,32},{32,48},{48,64},{64,80},{80,96},{96,112},{112,128},... | collective-permute-start | bytes 296 | tf_op jit(solution)/shard_map/ppermute | solution.py:21
  110.4 35.9 %collective-permute-start.4 = (f32[5,3072]{1,0:T(8,128)S(1)}, f32[5,3072]{1,0:T(8,128)S(1)}, u32[]{:S(2)}, u32[]{:S(2)}) collective-permute-start(f32[5,3072]{1,0:T(8,128)S(1)} %bitcast.309), channel_id=1, source_target_pairs={{0,16},{16,32},{32,48},{48,64},{64,80},{80,96},{96,112},{112,128},... | collective-permute-start | bytes 184328 | tf_op jit(solution)/shard_map/ppermute | solution.py:21
  144.9 34.0 %collective-permute-start.5 = (f32[5,3072]{1,0:T(8,128)S(1)}, f32[5,3072]{1,0:T(8,128)S(1)}, u32[]{:S(2)}, u32[]{:S(2)}) collective-permute-start(f32[5,3072]{1,0:T(8,128)S(1)} %bitcast.310), channel_id=1, source_target_pairs={{16,0},{32,16},{48,32},{64,48},{80,64},{96,80},{112,96},{128,112},... | collective-permute-start | bytes 184328 | tf_op jit(solution)/shard_map/ppermute | solution.py:21
  333.6 4.1 collective-permute-start.7
  334.9 3.1 collective-permute-start.6
  385.6 35.1 %collective-permute-start.8 = (f32[5,3072]{1,0:T(8,128)S(1)}, f32[5,3072]{1,0:T(8,128)S(1)}, u32[]{:S(2)}, u32[]{:S(2)}) collective-permute-start(f32[5,3072]{1,0:T(8,128)S(1)} %bitcast.311), channel_id=1, source_target_pairs={{0,16},{16,32},{32,48},{48,64},{64,80},{80,96},{96,112},{112,128},... | collective-permute-start | bytes 184328 | tf_op jit(solution)/shard_map/ppermute | solution.py:21
  419.4 32.4 %collective-permute-start.9 = (f32[5,3072]{1,0:T(8,128)S(1)}, f32[5,3072]{1,0:T(8,128)S(1)}, u32[]{:S(2)}, u32[]{:S(2)}) collective-permute-start(f32[5,3072]{1,0:T(8,128)S(1)} %bitcast.312), channel_id=1, source_target_pairs={{16,0},{32,16},{48,32},{64,48},{80,64},{96,80},{112,96},{128,112},... | collective-permute-start | bytes 184328 | tf_op jit(solution)/shard_map/ppermute | solution.py:21
